TPU v7x, 256 devices: a whole 4x4x8 slice. The times are simulated.
256 devices in a mesh: vocab: 32 (over y_hi, z, core), width: 8 (over x, y_lo).
Axes of the slice: x: 4, y: 4 (y_hi: 2, y_lo: 2; y = y_hi * 2 + y_lo), z: 8, core: 2. Of those that a mesh axis runs over, the one named last changes fastest.
Arguments:
- hidden: bfloat16 [256, 4608], P('vocab', 'width'), may hold values from -72 to 72
- pre_gain: float32 [4608], P('width'), may hold values from 0.1 to 1.9
- post_gain: float32 [4608], P('width'), may hold values from 0.1 to 1.9
- final_gain: float32 [4608], P('width'), may hold values from 0.1 to 1.9
- gate_weight: bfloat16 [4608, 18432], P('width', 'vocab'), may hold values from -0.09375 to 0.09375
- up_weight: bfloat16 [4608, 18432], P('width', 'vocab'), may hold values from -0.09375 to 0.09375
- down_weight: bfloat16 [18432, 4608], P('vocab', 'width'), may hold values from -2 to 2
- head_weight: bfloat16 [4608, 131072], P('width', 'vocab'), may hold values from -0.25 to 0.25
- token_ids: int32 [256], replicated, may hold values from 0 to 131071
- rewards: float32 [32], replicated, may hold values from -3 to 3
Outputs:
- grad_hidden: bfloat16 [256, 4608], P('vocab', 'width')
- grad_gate: bfloat16 [4608, 18432], P('width', 'vocab')
- grad_up: bfloat16 [4608, 18432], P('width', 'vocab')
- grad_down: bfloat16 [18432, 4608], P('vocab', 'width')
- grad_head: bfloat16 [4608, 131072], P('width', 'vocab')
- loss: float32 [], replicated
All inputs are finite; a program needn't handle non-finite values.
Results may differ from a plain program's by a relative error of at most 0.013.
Values may be sent and summed in bfloat16 or wider, within the bound.
No kernel may reach another device: no remote copies, remote signals or barrier semaphores. Data moves between devices by JAX's collectives and lax.ppermute only.
A program may use at most 64 MiB of HBM per device.

v0:
```python
import math
import jax
import jax.numpy as jnp
from jax import lax
from jax.sharding import PartitionSpec as P

CAP = 30
EPS = 1e-06
ROOT_TWO_PI = math.sqrt(2.0 / math.pi)


def gelu_value(value):
    inner = ROOT_TWO_PI * (value + 0.044715 * value * value * value)
    return 0.5 * value * (1.0 + jnp.tanh(inner))


def gelu_slope(value):
    bent = jnp.tanh(ROOT_TWO_PI * (value + 0.044715 * value * value * value))
    return 0.5 * (1.0 + bent) + 0.5 * value * (1.0 - bent * bent) * ROOT_TWO_PI * (
        1.0 + 3.0 * 0.044715 * value * value
    )


def contract(left, right, left_dim, right_dim):
    return lax.dot_general(
        left, right, (((left_dim,), (right_dim,)), ((), ())), preferred_element_type=jnp.float32
    )


def shards(
    hidden,
    pre_gain,
    post_gain,
    final_gain,
    gate_weight,
    up_weight,
    down_weight,
    head_weight,
    token_ids,
    rewards,
):
    tok_dev = hidden.shape[0]
    width_dev = hidden.shape[1]
    model = width_dev * lax.axis_size("width")
    vocab_index = lax.axis_index("vocab")
    width_index = lax.axis_index("width")
    own_start = vocab_index * tok_dev
    gathered = lax.all_gather(hidden, "vocab", axis=0, tiled=True)
    inputs = gathered.astype(jnp.float32)
    squares_pre = lax.psum(jnp.sum(inputs * inputs, axis=1), "width")
    scale_pre = lax.rsqrt(squares_pre / model + EPS)[:, None]
    normed = (inputs * scale_pre * pre_gain).astype(jnp.bfloat16)
    gate_part = jnp.dot(normed, gate_weight, preferred_element_type=jnp.float32)
    upward_part = jnp.dot(normed, up_weight, preferred_element_type=jnp.float32)
    gate, upward = lax.psum((gate_part, upward_part), "width")
    gelu_gate = gelu_value(gate)
    active = (gelu_gate * upward).astype(jnp.bfloat16)
    branch = lax.psum(jnp.dot(active, down_weight, preferred_element_type=jnp.float32), "vocab")
    branch_gain = branch * post_gain
    squares_post = lax.psum(jnp.sum(branch * branch, axis=1), "width")
    scale_post = lax.rsqrt(squares_post / model + EPS)[:, None]
    resid = inputs + scale_post * branch_gain
    squares_final = lax.psum(jnp.sum(resid * resid, axis=1), "width")
    scale_final = lax.rsqrt(squares_final / model + EPS)[:, None]
    final = (resid * scale_final * final_gain).astype(jnp.bfloat16)
    vocab_dev = head_weight.shape[1]
    sub_rows = vocab_dev // lax.axis_size("width")
    columns = head_weight
    logits = lax.psum_scatter(
        contract(columns, final, 0, 1), "width", scatter_dimension=0, tiled=True
    )
    capped = CAP * jnp.tanh(logits / CAP)
    first_column = vocab_index * vocab_dev + width_index * sub_rows
    column_ids = first_column + jnp.arange(sub_rows, dtype=jnp.int32)
    hits = column_ids[:, None] == token_ids[None, :]
    total, target = lax.psum(
        (jnp.sum(jnp.exp(capped - CAP), axis=0), jnp.sum(jnp.where(hits, capped, 0.0), axis=0)),
        ("vocab", "width"),
    )
    lognorm = CAP + jnp.log(total)
    logprob = target - lognorm
    weights = jnp.repeat(rewards, token_ids.shape[0] // rewards.shape[0])
    loss = -jnp.mean(weights * logprob)
    prob = jnp.exp(capped - lognorm[None, :])
    slope = 1.0 - (capped / CAP) ** 2
    delta = (-weights[None, :] * (hits.astype(jnp.float32) - prob) * slope).astype(jnp.bfloat16)
    piece = lax.all_gather(delta, "width", axis=0, tiled=True)
    columns = head_weight
    block = contract(final, piece, 0, 1)
    grad_cols = block
    grad_rows = contract(piece, columns, 0, 1)
    grad_cols, grad_rows = (grad_cols, grad_rows)
    grad_head = grad_cols.astype(jnp.bfloat16)
    grad_final = lax.psum(grad_rows, "vocab")
    weighted = grad_final * final_gain
    back_final = lax.psum(jnp.sum(weighted * resid, axis=1), "width")[:, None]
    grad_resid = scale_final * weighted - resid * scale_final**3 * back_final / model
    weighted_post = grad_resid * post_gain
    back_post = lax.psum(jnp.sum(weighted_post * branch, axis=1), "width")[:, None]
    grad_branch = (
        scale_post * weighted_post - branch * scale_post**3 * back_post / model
    ).astype(jnp.bfloat16)
    resid_rows = lax.dynamic_slice_in_dim(grad_resid, own_start, tok_dev, 0)
    grad_down = contract(active, grad_branch, 0, 0).astype(jnp.bfloat16)
    grad_active = lax.psum(contract(grad_branch, down_weight, 1, 1), "width")
    grad_gate_in = (grad_active * upward * gelu_slope(gate)).astype(jnp.bfloat16)
    grad_up_in = (grad_active * gelu_gate).astype(jnp.bfloat16)
    grad_gate = contract(normed, grad_gate_in, 0, 0).astype(jnp.bfloat16)
    grad_up = contract(normed, grad_up_in, 0, 0).astype(jnp.bfloat16)
    grad_normed = lax.psum_scatter(
        contract(grad_gate_in, gate_weight, 1, 1) + contract(grad_up_in, up_weight, 1, 1),
        "vocab",
        scatter_dimension=0,
        tiled=True,
    )
    own_inputs = hidden.astype(jnp.float32)
    own_scale = lax.dynamic_slice_in_dim(scale_pre, own_start, tok_dev, 0)
    weighted_pre = grad_normed * pre_gain
    back_pre = lax.psum(jnp.sum(weighted_pre * own_inputs, axis=1), "width")[:, None]
    grad_hidden = (
        resid_rows + own_scale * weighted_pre - own_inputs * own_scale**3 * back_pre / model
    ).astype(jnp.bfloat16)
    return (grad_hidden, grad_gate, grad_up, grad_down, grad_head, loss)


def solution(mesh):
    return jax.shard_map(
        shards,
        mesh=mesh,
        in_specs=(
            P("vocab", "width"),
            P("width"),
            P("width"),
            P("width"),
            P("width", "vocab"),
            P("width", "vocab"),
            P("vocab", "width"),
            P("width", "vocab"),
            P(),
            P(),
        ),
        out_specs=(
            P("vocab", "width"),
            P("width", "vocab"),
            P("width", "vocab"),
            P("vocab", "width"),
            P("width", "vocab"),
            P(),
        ),
        check_vma=False,
    )
```

profile of v0, /device:TPU:16, one launch (start us, length us, event | category | flops | bytes accessed | tf_op | source)
XLA Modules:
  0.0 1352.1 jit_solution(14111036055207850782)
XLA Ops:
  7.2 43.3 %all_gather.6 = bf16[256,576]{1,0:T(8,128)(2,1)S(1)} all-gather(bf16[8,576]{1,0:T(8,128)(2,1)} %param.10), channel_id=1, replica_groups=mesh['vocab'=32,'width'=8] {'vocab'}, dimensions={0}, use_global_device_ids=true | all-gather | bytes 304128 | tf_op jit(solution)/shard_map/all_gather | solution.py:48
  50.6 20.3 %psum.91 = f32[256]{0:T(256)S(1)} all-reduce(f32[256]{0:T(256)S(1)} %fusion), channel_id=1, replica_groups=mesh['vocab'=32,'width'=8] {'width'}, use_global_device_ids=true, to_apply=%region_1.0 | all-reduce | flops 256 | bytes 2048 | tf_op jit(solution)/shard_map/psum | solution.py:50
  71.0 2.5 fusion.23
  73.5 2.5 fusion.25
  76.0 77.8 %all-reduce.17.cloned.1.call-done = (f32[256,576]{0,1:T(8,128)}, f32[256,576]{0,1:T(8,128)}) async-done(((f32[256,576]{0,1:T(8,128)}, f32[256,576]{0,1:T(8,128)}), (f32[256,576]{0,1:T(8,128)}, f32[256,576]{0,1:T(8,128)})) %all-reduce.17.cloned.1.call-update) | async-done | bytes 1179664 | tf_op jit(solution)/shard_map/psum | solution.py:55
  153.8 1.4 multiply_convert_fusion.2
  156.0 1.3 fusion.27
  157.3 258.8 %all-reduce.9.cloned.1.call-done = f32[256,576]{1,0:T(8,128)} async-done(((f32[256,576]{1,0:T(8,128)}), f32[256,576]{1,0:T(8,128)}) %all-reduce.9.cloned.1.call-update) | async-done | bytes 589840 | tf_op jit(solution)/shard_map/psum | solution.py:58
  417.4 19.3 %psum.95 = f32[256]{0:T(256)S(1)} all-reduce(f32[256]{0:T(256)S(1)} %multiply_reduce_fusion.3), channel_id=1, replica_groups=mesh['vocab'=32,'width'=8] {'width'}, use_global_device_ids=true, to_apply=%region_6.0 | all-reduce | flops 256 | bytes 2048 | tf_op jit(solution)/shard_map/psum | solution.py:60
  436.7 1.4 multiply_reduce_fusion.2
  438.0 16.0 %psum.96 = f32[256]{0:T(256)S(1)} all-reduce(f32[256]{0:T(256)S(1)} %get-tuple-element.34), channel_id=1, replica_groups=mesh['vocab'=32,'width'=8] {'width'}, use_global_device_ids=true, to_apply=%region_8.0 | all-reduce | flops 256 | bytes 2048 | tf_op jit(solution)/shard_map/psum | solution.py:63
  454.0 6.2 convolution_bitcast_fusion
  461.1 86.4 %reduce-scatter.3.cloned.1.call-done = f32[512,256]{0,1:T(8,128)} async-done(((f32[4096,256]{0,1:T(8,128)}), f32[512,256]{0,1:T(8,128)}) %reduce-scatter.3.cloned.1.call-update) | async-done | bytes 524304 | tf_op jit(solution)/shard_map/reduce_scatter | solution.py:69
  547.5 1.3 fusion.14
  548.8 75.9 %all-reduce.1 = (f32[256]{0:T(256)S(1)}, f32[256]{0:T(256)S(1)}) all-reduce(f32[256]{0:T(256)S(1)} %get-tuple-element.25, f32[256]{0:T(256)S(1)} %get-tuple-element.24), channel_id=1, replica_groups=mesh['vocab'=32,'width'=8] {'vocab','width'}, use_global_device_ids=true, to_apply=%region_11.12 | all-reduce | flops 512 | bytes 4096 | tf_op jit(solution)/shard_map/psum | solution.py:76
  625.4 2.0 fusion.13
  627.5 51.3 %all-gather.2.cloned.1.call-done = bf16[4096,256]{0,1:T(8,128)(2,1)} async-done(((bf16[512,256]{0,1:T(8,128)(2,1)}), bf16[4096,256]{0,1:T(8,128)(2,1)}) %all-gather.2.cloned.1.call-update) | async-done | bytes 2097168 | tf_op jit(solution)/shard_map/all_gather | solution.py:87
  678.8 5.6 fusion.28
  684.5 259.4 %all-reduce.11.cloned.1.call-done = f32[256,576]{1,0:T(8,128)} async-done(((f32[256,576]{1,0:T(8,128)}), f32[256,576]{1,0:T(8,128)}) %all-reduce.11.cloned.1.call-update) | async-done | bytes 589840 | tf_op jit(solution)/shard_map/psum | solution.py:94
  945.1 19.3 %psum.99 = f32[256]{0:T(256)S(1)} all-reduce(f32[256]{0:T(256)S(1)} %multiply_reduce_fusion.1), channel_id=1, replica_groups=mesh['vocab'=32,'width'=8] {'width'}, use_global_device_ids=true, to_apply=%region_14.15 | all-reduce | flops 256 | bytes 2048 | tf_op jit(solution)/shard_map/psum | solution.py:96
  964.4 2.3 multiply_reduce_fusion
  966.7 15.9 %psum.100 = f32[256]{0:T(256)S(1)} all-reduce(f32[256]{0:T(256)S(1)} %get-tuple-element.32), channel_id=1, replica_groups=mesh['vocab'=32,'width'=8] {'width'}, use_global_device_ids=true, to_apply=%region_16.17 | all-reduce | flops 256 | bytes 2048 | tf_op jit(solution)/shard_map/psum | solution.py:99
  982.6 1.3 subtract_convert_fusion
  987.4 72.3 %all-reduce.13.cloned.1.call-done = f32[256,576]{0,1:T(8,128)} async-done(((f32[256,576]{0,1:T(8,128)}), f32[256,576]{0,1:T(8,128)}) %all-reduce.13.cloned.1.call-update) | async-done | bytes 589840 | tf_op jit(solution)/shard_map/psum | solution.py:105
  1059.7 1.9 multiply_convert_fusion.1
  1063.8 5.3 convolution_convert_fusion
  1069.1 1.3 convolution_convert_fusion.1
  1070.4 1.4 convolution_convert_fusion.2
  1071.8 249.0 %all-reduce.15.cloned.1.call-done = f32[256,576]{0,1:T(8,128)} async-done(((f32[256,576]{0,1:T(8,128)}), f32[256,576]{0,1:T(8,128)}) %all-reduce.15.cloned.1.call-update) | async-done | bytes 589840
  1322.1 1.4 convolution_convert_fusion.3
  1323.5 19.2 %psum.102 = f32[8]{0:T(128)S(1)} all-reduce(f32[8]{0:T(128)S(1)} %fusion.20), channel_id=1, replica_groups=mesh['vocab'=32,'width'=8] {'width'}, use_global_device_ids=true, to_apply=%region_20.21 | all-reduce | flops 8 | bytes 64 | tf_op jit(solution)/shard_map/psum | solution.py:119
  1342.7 1.4 fusion.19
  (59 shorter events, 10.6 us)
Async XLA Ops:
  7.2 148.8 %copy-start = (bf16[576,576]{1,0:T(8,128)(2,1)S(1)}, bf16[576,576]{1,0:T(8,128)(2,1)}, u32[]{:S(2)}) copy-start(bf16[576,576]{1,0:T(8,128)(2,1)} %param.16) | copy-start | bytes 1990660
  7.2 146.6 %all-reduce.17.cloned.1.call-start = ((), (), s32[]{:S(2)}) async-start(), calls=%async_computation.7 | async-start | bytes 2359296 | tf_op jit(solution)/shard_map/psum | solution.py:55
  71.0 365.7 %copy-start.9 = (f32[576]{0:T(1024)S(1)}, f32[576]{0:T(1024)}, u32[]{:S(2)}) copy-start(f32[576]{0:T(1024)} %param.12) | copy-start | bytes 6916
  73.5 380.6 %copy-start.6 = (f32[576]{0:T(1024)S(1)}, f32[576]{0:T(1024)}, u32[]{:S(2)}) copy-start(f32[576]{0:T(1024)} %param.13) | copy-start | bytes 6916
  76.0 340.2 %all-reduce.9.cloned.1.call-start = ((), (), s32[]{:S(2)}) async-start(), calls=%async_computation.1 | async-start | bytes 1310720 | tf_op jit(solution)/shard_map/psum | solution.py:58
  155.2 0.7 copy-start.4
  157.3 390.2 %reduce-scatter.3.cloned.1.call-start = ((), (), s32[]{:S(2)}) async-start(), calls=%async_computation.2 | async-start | bytes 4718592 | tf_op jit(solution)/shard_map/reduce_scatter | solution.py:69
  460.2 0.7 copy-start.11
  460.2 87.3 %copy-start.10 = (s32[256]{0:T(256)S(1)}, s32[256]{0:T(256)}, u32[]{:S(2)}) copy-start(s32[256]{0:T(256)} %param.18) | copy-start | bytes 3076
  460.2 218.6 %all-gather.2.cloned.1.call-start = ((), (), s32[]{:S(2)}) async-start(), calls=%async_computation.3 | async-start | bytes 2359296 | tf_op jit(solution)/shard_map/all_gather | solution.py:87
  627.4 337.0 %copy-start.1 = (f32[256,576]{1,0:T(8,128)S(1)}, f32[256,576]{1,0:T(8,128)}, u32[]{:S(2)}) copy-start(f32[256,576]{1,0:T(8,128)} %all-reduce.9.cloned.1.call-done) | copy-start | bytes 1769476
  627.4 316.5 %all-reduce.11.cloned.1.call-start = ((), (), s32[]{:S(2)}) async-start(), calls=%async_computation.4 | async-start | bytes 1310720 | tf_op jit(solution)/shard_map/psum | solution.py:94
  684.4 301.0 %copy-start.12 = (u32[256]{0:T(256)S(1)}, u32[256]{0:T(256)}, u32[]{:S(2)}) copy-start(u32[256]{0:T(256)} %constant.59) | copy-start | bytes 3076
  684.5 375.2 %all-reduce.13.cloned.1.call-start = ((), (), s32[]{:S(2)}) async-start(), calls=%async_computation.5 | async-start | bytes 1179648 | tf_op jit(solution)/shard_map/psum | solution.py:105
  964.4 97.2 %copy-start.2 = (bf16[576,576]{1,0:T(8,128)(2,1)S(1)}, bf16[576,576]{1,0:T(8,128)(2,1)}, u32[]{:S(2)}) copy-start(bf16[576,576]{1,0:T(8,128)(2,1)} %param.14) | copy-start | bytes 1990660
  985.2 335.5 %all-reduce.15.cloned.1.call-start = ((), (), s32[]{:S(2)}) async-start(), calls=%async_computation.6 | async-start | bytes 1179648
  1059.7 2.5 copy-start.3
  1063.7 5.4 copy-start.5
  1063.7 6.6 copy-start.7
  1063.8 258.2 %copy-start.8 = (bf16[8,576]{1,0:T(8,128)(2,1)S(1)}, bf16[8,576]{1,0:T(8,128)(2,1)}, u32[]{:S(2)}) copy-start(bf16[8,576]{1,0:T(8,128)(2,1)} %param.10) | copy-start | bytes 27652
Sparse Core Ops, SparseCore 0:
  76.1 77.6 all-reduce.16
  157.4 258.7 all-reduce.8
  460.4 87.0 reduce-scatter.2
  627.5 51.2 all-gather.1
  684.6 259.2 all-reduce.10
  985.3 74.3 all-reduce.12
  1063.8 256.8 all-reduce.14
where the time goes:
time: 1350 us
  waiting for transfers between devices  1060 us (79%)
  blocking collectives  229 us (17%)
  matrix products  29.8 us (2%)
  between operations  16.7 us (1%)
  other arithmetic  16.5 us (1%)
    psum x1, waiting for transfers between devices, shards(): grad_final = lax.psum(grad_rows, 'vocab')  259 us
    psum x1, waiting for transfers between devices, shards(): lax.psum(jnp.dot(active, down_weight, preferred_element_type=jnp.float32)...  259 us
    unnamed x8, waiting for transfers between devices  249 us
    reduce_scatter x1, waiting for transfers between devices, shards(): lax.psum_scatter(contract(columns, final, 0, 1), 'width', scatter_dimensi...  86.4 us
    psum x1, waiting for transfers between devices, shards(): gate, upward = lax.psum((gate_part, upward_part), 'width')  77.8 us
    psum x1, blocking collectives, shards(): lax.psum((jnp.sum(jnp.exp(capped - CAP), axis=0), jnp.sum(jnp.where(hits,...  75.9 us
    psum x1, waiting for transfers between devices, shards(): grad_active = lax.psum(contract(grad_branch, down_weight, 1, 1), 'width')  72.3 us
    all_gather x1, waiting for transfers between devices, shards(): piece = lax.all_gather(delta, 'width', axis=0, tiled=True)  51.3 us
  transfers between devices with their start and end apart: 7, of which 7 were waited for; matrix products, arithmetic and copies ran while one was open for 1% of the time, Pallas kernels for 0%

commit v1 on v0

--- a/solution.py
+++ b/solution.py
@@ -55,7 +55,10 @@
     gate, upward = lax.psum((gate_part, upward_part), "width")
     gelu_gate = gelu_value(gate)
     active = (gelu_gate * upward).astype(jnp.bfloat16)
-    branch = lax.psum(jnp.dot(active, down_weight, preferred_element_type=jnp.float32), "vocab")
+    branch = jnp.sum(
+        lax.all_gather(jnp.dot(active, down_weight, preferred_element_type=jnp.float32), "vocab"),
+        axis=0,
+    )
     branch_gain = branch * post_gain
     squares_post = lax.psum(jnp.sum(branch * branch, axis=1), "width")
     scale_post = lax.rsqrt(squares_post / model + EPS)[:, None]

time: 1350 us -> 1280 us (0.948)
  waiting for transfers between devices: 1060 us -> 962 us
  local copies, waits for them, and re-layouts: 4.32 us -> 20.8 us
    psum x1 -> x0, waiting for transfers between devices: 259 us -> none  [shards(): lax.psum(jnp.dot(active, down_weight, preferred_element_type=jnp.float32)...]
    all_gather x0 -> x1, waiting for transfers between devices: none -> 163 us  [shards(): lax.all_gather(jnp.dot(active, down_weight, preferred_element_type=jnp.fl...]
    unnamed x28 -> x25, local copies, waits for them, and re-layouts: 3.01 us -> 19.3 us
where the time goes in v1:
time: 1280 us
  waiting for transfers between devices  962 us (75%)
  blocking collectives  230 us (18%)
  matrix products  30.8 us (2%)
  other arithmetic  23.8 us (2%)
  local copies, waits for them, and re-layouts  20.8 us (2%)
  between operations  16.8 us (1%)
    psum x1, waiting for transfers between devices, shards(): grad_final = lax.psum(grad_rows, 'vocab')  259 us
    unnamed x8, waiting for transfers between devices  249 us
    all_gather x1, waiting for transfers between devices, shards(): lax.all_gather(jnp.dot(active, down_weight, preferred_element_type=jnp.fl...  163 us
    reduce_scatter x1, waiting for transfers between devices, shards(): lax.psum_scatter(contract(columns, final, 0, 1), 'width', scatter_dimensi...  88.8 us
    psum x1, waiting for transfers between devices, shards(): gate, upward = lax.psum((gate_part, upward_part), 'width')  77.7 us
    psum x1, blocking collectives, shards(): lax.psum((jnp.sum(jnp.exp(capped - CAP), axis=0), jnp.sum(jnp.where(hits,...  76.1 us
    psum x1, waiting for transfers between devices, shards(): grad_active = lax.psum(contract(grad_branch, down_weight, 1, 1), 'width')  72.6 us
    all_gather x1, waiting for transfers between devices, shards(): piece = lax.all_gather(delta, 'width', axis=0, tiled=True)  51.3 us
  transfers between devices with their start and end apart: 7, of which 7 were waited for; matrix products, arithmetic and copies ran while one was open for 1% of the time, Pallas kernels for 0%

profile of v1, /device:TPU:16, one launch (start us, length us, event | category | flops | bytes accessed | tf_op | source)
XLA Modules:
  0.0 1283.9 jit_solution(6386753980862892856)
XLA Ops:
  7.2 43.3 %all_gather.12 = bf16[256,576]{1,0:T(8,128)(2,1)S(1)} all-gather(bf16[8,576]{1,0:T(8,128)(2,1)} %param.10), channel_id=1, replica_groups=mesh['vocab'=32,'width'=8] {'vocab'}, dimensions={0}, use_global_device_ids=true | all-gather | bytes 304128 | tf_op jit(solution)/shard_map/all_gather | solution.py:48
  50.6 20.3 %psum.84 = f32[256]{0:T(256)S(1)} all-reduce(f32[256]{0:T(256)S(1)} %fusion), channel_id=1, replica_groups=mesh['vocab'=32,'width'=8] {'width'}, use_global_device_ids=true, to_apply=%region_1.0 | all-reduce | flops 256 | bytes 2048 | tf_op jit(solution)/shard_map/psum | solution.py:50
  71.0 2.5 fusion.25
  73.4 2.5 fusion.23
  76.0 77.7 %all-reduce.14.cloned.1.call-done = (f32[256,576]{0,1:T(8,128)}, f32[256,576]{0,1:T(8,128)}) async-done(((f32[256,576]{0,1:T(8,128)}, f32[256,576]{0,1:T(8,128)}), (f32[256,576]{0,1:T(8,128)}, f32[256,576]{0,1:T(8,128)})) %all-reduce.14.cloned.1.call-update) | async-done | bytes 1179664 | tf_op jit(solution)/shard_map/psum | solution.py:55
  153.7 1.4 multiply_convert_fusion.2
  156.5 163.3 %all-gather.6.cloned.1.call-done = f32[8192,576]{0,1:T(8,128)} async-done(((f32[256,576]{0,1:T(8,128)}), f32[8192,576]{0,1:T(8,128)}) %all-gather.6.cloned.1.call-update) | async-done | bytes 18874384 | tf_op jit(solution)/shard_map/all_gather | solution.py:59
  319.8 17.6 %copy.57 = f32[72,8,32,256]{3,2,1,0:T(8,128)} copy(f32[72,8,32,256]{3,1,2,0:T(8,128)} %bitcast.28) | data formatting | bytes 37748736
  337.4 9.7 bitcast_reduce_fusion
  347.4 19.3 %psum.87 = f32[256]{0:T(256)S(1)} all-reduce(f32[256]{0:T(256)S(1)} %multiply_reduce_fusion.3), channel_id=1, replica_groups=mesh['vocab'=32,'width'=8] {'width'}, use_global_device_ids=true, to_apply=%region_6.0 | all-reduce | flops 256 | bytes 2048 | tf_op jit(solution)/shard_map/psum | solution.py:63
  367.0 16.0 %psum.88 = f32[256]{0:T(256)S(1)} all-reduce(f32[256]{0:T(256)S(1)} %get-tuple-element.34), channel_id=1, replica_groups=mesh['vocab'=32,'width'=8] {'width'}, use_global_device_ids=true, to_apply=%region_8.0 | all-reduce | flops 256 | bytes 2048 | tf_op jit(solution)/shard_map/psum | solution.py:66
  383.0 6.2 convolution_bitcast_fusion
  389.5 88.8 %reduce-scatter.3.cloned.1.call-done = f32[512,256]{0,1:T(8,128)} async-done(((f32[4096,256]{0,1:T(8,128)}), f32[512,256]{0,1:T(8,128)}) %reduce-scatter.3.cloned.1.call-update) | async-done | bytes 524304 | tf_op jit(solution)/shard_map/reduce_scatter | solution.py:72
  478.2 1.3 fusion.14
  479.6 76.1 %all-reduce.1 = (f32[256]{0:T(256)S(1)}, f32[256]{0:T(256)S(1)}) all-reduce(f32[256]{0:T(256)S(1)} %get-tuple-element.25, f32[256]{0:T(256)S(1)} %get-tuple-element.24), channel_id=1, replica_groups=mesh['vocab'=32,'width'=8] {'vocab','width'}, use_global_device_ids=true, to_apply=%region_11.12 | all-reduce | flops 512 | bytes 4096 | tf_op jit(solution)/shard_map/psum | solution.py:79
  556.3 2.0 fusion.13
  558.4 51.3 %all-gather.4.cloned.1.call-done = bf16[4096,256]{0,1:T(8,128)(2,1)} async-done(((bf16[512,256]{0,1:T(8,128)(2,1)}), bf16[4096,256]{0,1:T(8,128)(2,1)}) %all-gather.4.cloned.1.call-update) | async-done | bytes 2097168 | tf_op jit(solution)/shard_map/all_gather | solution.py:90
  609.7 5.6 fusion.28
  615.5 259.1 %all-reduce.8.cloned.1.call-done = f32[256,576]{1,0:T(8,128)} async-done(((f32[256,576]{1,0:T(8,128)}), f32[256,576]{1,0:T(8,128)}) %all-reduce.8.cloned.1.call-update) | async-done | bytes 589840 | tf_op jit(solution)/shard_map/psum | solution.py:97
  875.8 19.4 %psum.91 = f32[256]{0:T(256)S(1)} all-reduce(f32[256]{0:T(256)S(1)} %multiply_reduce_fusion.1), channel_id=1, replica_groups=mesh['vocab'=32,'width'=8] {'width'}, use_global_device_ids=true, to_apply=%region_14.15 | all-reduce | flops 256 | bytes 2048 | tf_op jit(solution)/shard_map/psum | solution.py:99
  895.2 2.2 multiply_reduce_fusion
  897.4 15.9 %psum.92 = f32[256]{0:T(256)S(1)} all-reduce(f32[256]{0:T(256)S(1)} %get-tuple-element.32), channel_id=1, replica_groups=mesh['vocab'=32,'width'=8] {'width'}, use_global_device_ids=true, to_apply=%region_16.17 | all-reduce | flops 256 | bytes 2048 | tf_op jit(solution)/shard_map/psum | solution.py:102
  913.3 1.3 subtract_convert_fusion
  917.9 72.6 %all-reduce.10.cloned.1.call-done = f32[256,576]{0,1:T(8,128)} async-done(((f32[256,576]{0,1:T(8,128)}), f32[256,576]{0,1:T(8,128)}) %all-reduce.10.cloned.1.call-update) | async-done | bytes 589840 | tf_op jit(solution)/shard_map/psum | solution.py:108
  990.5 1.9 multiply_convert_fusion.1
  992.9 1.6 convolution_add_fusion
  995.6 5.3 convolution_convert_fusion
  1002.2 1.4 convolution_convert_fusion.2
  1003.6 249.0 %all-reduce.12.cloned.1.call-done = f32[256,576]{0,1:T(8,128)} async-done(((f32[256,576]{0,1:T(8,128)}), f32[256,576]{0,1:T(8,128)}) %all-reduce.12.cloned.1.call-update) | async-done | bytes 589840
  1253.9 1.4 convolution_convert_fusion.3
  1255.3 19.2 %psum.94 = f32[8]{0:T(128)S(1)} all-reduce(f32[8]{0:T(128)S(1)} %fusion.20), channel_id=1, replica_groups=mesh['vocab'=32,'width'=8] {'width'}, use_global_device_ids=true, to_apply=%region_20.21 | all-reduce | flops 8 | bytes 64 | tf_op jit(solution)/shard_map/psum | solution.py:122
  1274.6 1.4 fusion.19
  (58 shorter events, 10.6 us)
Async XLA Ops:
  7.2 147.9 %copy-start = (bf16[576,576]{1,0:T(8,128)(2,1)S(1)}, bf16[576,576]{1,0:T(8,128)(2,1)}, u32[]{:S(2)}) copy-start(bf16[576,576]{1,0:T(8,128)(2,1)} %param.16) | copy-start | bytes 1990660
  7.2 146.5 %all-reduce.14.cloned.1.call-start = ((), (), s32[]{:S(2)}) async-start(), calls=%async_computation.7 | async-start | bytes 2359296 | tf_op jit(solution)/shard_map/psum | solution.py:55
  75.9 243.9 %all-gather.6.cloned.1.call-start = ((), (), s32[]{:S(2)}) async-start(), calls=%async_computation.5 | async-start | bytes 19464192 | tf_op jit(solution)/shard_map/all_gather | solution.py:59
  155.1 164.7 %copy-start.2 = (bf16[256,576]{0,1:T(8,128)(2,1)}, bf16[256,576]{0,1:T(8,128)(2,1)S(1)}, u32[]{:S(2)}) copy-start(bf16[256,576]{0,1:T(8,128)(2,1)S(1)} %multiply_convert_fusion.2) | copy-start | bytes 884740
  156.4 321.8 %reduce-scatter.3.cloned.1.call-start = ((), (), s32[]{:S(2)}) async-start(), calls=%async_computation.1 | async-start | bytes 4718592 | tf_op jit(solution)/shard_map/reduce_scatter | solution.py:72
  337.4 29.3 %copy-start.7 = (f32[576]{0:T(1024)S(1)}, f32[576]{0:T(1024)}, u32[]{:S(2)}) copy-start(f32[576]{0:T(1024)} %param.12) | copy-start | bytes 6916
  337.4 45.6 %copy-start.4 = (f32[576]{0:T(1024)S(1)}, f32[576]{0:T(1024)}, u32[]{:S(2)}) copy-start(f32[576]{0:T(1024)} %param.13) | copy-start | bytes 6916
  382.9 6.3 copy-start.9
  382.9 95.3 %copy-start.8 = (s32[256]{0:T(256)S(1)}, s32[256]{0:T(256)}, u32[]{:S(2)}) copy-start(s32[256]{0:T(256)} %param.18) | copy-start | bytes 3076
  389.2 220.5 %all-gather.4.cloned.1.call-start = ((), (), s32[]{:S(2)}) async-start(), calls=%async_computation.2 | async-start | bytes 2359296 | tf_op jit(solution)/shard_map/all_gather | solution.py:90
  558.4 316.2 %all-reduce.8.cloned.1.call-start = ((), (), s32[]{:S(2)}) async-start(), calls=%async_computation.3 | async-start | bytes 1310720 | tf_op jit(solution)/shard_map/psum | solution.py:97
  615.4 300.6 %copy-start.10 = (u32[256]{0:T(256)S(1)}, u32[256]{0:T(256)}, u32[]{:S(2)}) copy-start(u32[256]{0:T(256)} %constant.59) | copy-start | bytes 3076
  615.4 375.1 %all-reduce.10.cloned.1.call-start = ((), (), s32[]{:S(2)}) async-start(), calls=%async_computation.4 | async-start | bytes 1179648 | tf_op jit(solution)/shard_map/psum | solution.py:108
  875.8 116.6 %copy-start.1 = (bf16[576,576]{1,0:T(8,128)(2,1)S(1)}, bf16[576,576]{1,0:T(8,128)(2,1)}, u32[]{:S(2)}) copy-start(bf16[576,576]{1,0:T(8,128)(2,1)} %param.14) | copy-start | bytes 1990660
  915.9 336.6 %all-reduce.12.cloned.1.call-start = ((), (), s32[]{:S(2)}) async-start(), calls=%async_computation.6 | async-start | bytes 1179648
  995.6 5.4 copy-start.3
  995.6 6.6 copy-start.5
  995.6 258.2 %copy-start.6 = (bf16[8,576]{1,0:T(8,128)(2,1)S(1)}, bf16[8,576]{1,0:T(8,128)(2,1)}, u32[]{:S(2)}) copy-start(bf16[8,576]{1,0:T(8,128)(2,1)} %param.10) | copy-start | bytes 27652
Sparse Core Ops, SparseCore 0:
  76.1 77.5 all-reduce.13
  156.8 162.9 all-gather.5
  389.3 88.8 reduce-scatter.2
  558.5 51.2 all-gather.3
  615.5 258.9 all-reduce.7
  916.0 74.4 all-reduce.9
  995.7 256.8 all-reduce.11
